TPU v7x, 256 devices: a whole 4x4x8 slice. The times are simulated.
256 devices in a mesh: gx: 64 (over z, x, core), gy: 4 (over y).
Axes of the slice: x: 4, y: 4, z: 8, core: 2. Of those that a mesh axis runs over, the one named last changes fastest.
Arguments:
- conserved: float32 [5, 1024, 64, 512], P(None, 'gx', 'gy'), as said below
- shock_flags: int32 [64, 4, 32], P('gx', 'gy'), may hold values from 0 to 1, as said below
Outputs:
- advanced: float32 [5, 1024, 64, 512], P(None, 'gx', 'gy')
- tendency: float32 [5, 1024, 64, 512], P(None, 'gx', 'gy')
Inputs may be any that keep to these rules, and one draw needn't show every extreme that they name: `shock_flags`: for every block index along the second dimension, the blocks flagged 1 lie within a quarter of the 64 block columns along the first dimension, consecutive when counted cyclically. `conserved`: density and pressure are positive in every cell.
All inputs are finite; a program needn't handle non-finite values.
Results may differ from a plain program's by a relative error of at most 0.0003.
Values sent between devices are 32-bit elements; how exact they have to be, the bound alone decides.
No kernel may reach another device: no remote copies, remote signals or barrier semaphores. Data moves between devices by JAX's collectives and lax.ppermute only.
A program may use at most 128 MiB of HBM per device.

v0:
```python
import functools

import jax
import jax.numpy as jnp
from jax import lax
from jax.experimental import pallas as pl
from jax.experimental.pallas import tpu as pltpu
from jax.sharding import PartitionSpec as P

GAMMA = 1.4
GAMMA_LESS = 0.4
COURANT = 0.4
EPSILON = 1e-06
LANES = 128
ROWS = 8
TINY = 1e-37


def cell_values(density, mom, energy, normal):
    inv = 1.0 / density
    inv_half = 0.5 * inv
    half_vel = [m * inv_half for m in mom]
    kinetic = mom[0] * half_vel[0] + mom[1] * half_vel[1] + mom[2] * half_vel[2]
    pressure = GAMMA_LESS * (energy - kinetic)
    total = energy + pressure
    sound_sq = GAMMA * pressure * inv
    sound = sound_sq * lax.rsqrt(jnp.maximum(sound_sq, TINY))
    half_normal = half_vel[normal]
    flux = [0.5 * mom[normal]]
    for other in range(3):
        part = mom[other] * half_normal
        flux.append(part + 0.5 * pressure if other == normal else part)
    flux.append(total * half_normal)
    means = [half_vel[n] for n in pair_order(normal)] + [total * inv_half]
    return flux, means, jnp.abs(half_normal) + 0.5 * sound


def pair_order(normal):
    return [normal] + [other for other in range(3) if other != normal]


def recon_rest(d1, d2, d3, d4):
    t1 = d2 - d1
    t2 = d3 - d2
    t3 = d4 - d3
    d2s = 0.75 * d2
    d3s = 0.75 * d3
    p2 = d2s * d2 + 0.75 * EPSILON
    p3 = d3s * d3 + 0.75 * EPSILON
    r0 = 1.0 / (t1 * (t1 + d2s) + p2)
    r1 = 1.0 / (t2 * (t2 + d2s) + p2)
    r2 = 1.0 / (t3 * (t3 - d3s) + p3)
    z0 = r0 * r0
    z1 = r1 * r1
    z2 = 1.5 * (r2 * r2)
    num = z0 * (t2 - t1) + z2 * (t3 - t2)
    den = z2 + (0.5 * z0 + 3.0 * z1)
    return num * (1.0 / den)


def central_rest(d_flux):
    return [
        (1.0 / 30.0) * ((d_flux[4][c] - d_flux[0][c]) - 7.0 * (d_flux[3][c] - d_flux[1][c]))
        for c in range(5)
    ]


def face_terms(means):
    a, b, e, h = means
    k = 0.5 * (a * a + b * b + e * e)
    s_sq = GAMMA_LESS * (h - k)
    inv_s = lax.rsqrt(s_sq)
    return [a, b, e, h, k, s_sq * inv_s, (0.5 * GAMMA_LESS) * (inv_s * inv_s), 0.5 * inv_s]


def face_order(normal):
    return [0] + [1 + n for n in pair_order(normal)] + [4]


def weno_waves(d_flux, d_state, terms, alpha, normal):
    order = face_order(normal)
    a, b, e, _, k, _, half_g, half_inv = terms

    def project(x):
        x1 = x[1] - a * x[0]
        x2 = x[2] - b * x[0]
        x3 = x[3] - e * x[0]
        y = half_g * (x[4] - a * x1 - b * x2 - e * x3 - k * x[0])
        z = half_inv * x1
        return [y - z, x[0] - (y + y), x2, x3, y + z]

    up = []
    down = []
    for step in range(5):
        scaled = [alpha * d_state[step][c] for c in order]
        flux = [d_flux[step][c] for c in order]
        up.append([f + q for f, q in zip(flux, scaled)] if step < 4 else None)
        down.append([f - q for f, q in zip(flux, scaled)] if step > 0 else None)
    linear = [(up[1][c] - down[3][c]) - (up[2][c] - down[2][c]) for c in range(5)]
    up = [project(x) if x is not None else None for x in up]
    down = [project(x) if x is not None else None for x in down]
    waves = [
        recon_rest(up[0][c], up[1][c], up[2][c], up[3][c])
        - recon_rest(down[4][c], down[3][c], down[2][c], down[1][c])
        for c in range(5)
    ]
    return linear, waves


def weno_rest(linear, waves, terms, normal):
    a, b, e, h, k, s = terms[:6]
    outer = waves[0] + waves[4]
    shared = outer + waves[1]
    swing = s * (waves[4] - waves[0])
    back = [
        shared,
        a * shared + swing,
        b * shared + waves[2],
        e * shared + waves[3],
        h * outer + k * waves[1] + b * waves[2] + e * waves[3] + a * swing,
    ]
    rest = [None] * 5
    for position, component in enumerate(face_order(normal)):
        rest[component] = (1.0 / 6.0) * (linear[position] - back[position])
    return rest


class Line:
    def __init__(self, refs, normal, unit):
        self.v_ref, self.p_ref, self.w_ref, self.f_ref = refs
        self.normal = normal
        self.unit = unit

    def rows(self, i, off=0):
        start = i * ROWS + off * self.unit
        if (off * self.unit) % ROWS == 0 and not isinstance(i, int):
            start = pl.multiple_of(start, ROWS)
        return pl.ds(start, ROWS)

    def cell(self, i, q):
        n = self.normal
        flux, means, wave = cell_values(q[0], q[1:4], q[4], n)
        now = list(q) + flux + means + [wave]
        here, prev = self.rows(i), self.rows(i, -1)
        for v in range(15):
            self.v_ref[v, here, :] = now[v]
        before = [self.v_ref[v, prev, :] for v in range(15)]
        for v in range(10):
            self.p_ref[v, here, :] = now[v] - before[v]
        self.p_ref[10, here, :] = jnp.maximum(now[14], before[14])
        terms = face_terms([now[v] + before[v] for v in range(10, 14)])
        for v in range(8):
            self.p_ref[11 + v, here, :] = terms[v]

    def pair(self, v, j, off=0):
        return self.p_ref[v, self.rows(j, off), :]

    def fluxes(self, j):
        return [[self.pair(5 + c, j, k - 2) for c in range(5)] for k in range(5)]

    def central(self, j, d_flux):
        for c, value in enumerate(central_rest(d_flux)):
            self.f_ref[c, self.rows(j), :] = value

    def waves(self, j, d_flux):
        d_state = [[self.pair(c, j, k - 2) for c in range(5)] for k in range(5)]
        terms = [self.pair(11 + v, j) for v in range(8)]
        alpha = jnp.maximum(jnp.maximum(self.pair(10, j, -2), self.pair(10, j)), self.pair(10, j, 2))
        linear, waves = weno_waves(d_flux, d_state, terms, alpha, self.normal)
        for c in range(5):
            self.w_ref[c, self.rows(j), :] = linear[c]
            self.w_ref[5 + c, self.rows(j), :] = waves[c]

    def face(self, j):
        both = [self.w_ref[c, self.rows(j), :] for c in range(10)]
        terms = [self.pair(11 + v, j) for v in range(6)]
        for c, value in enumerate(weno_rest(both[:5], both[5:], terms, self.normal)):
            self.f_ref[5 + c, self.rows(j), :] = value

    def change(self, j, first):
        here, following = self.rows(j), self.rows(j, 1)
        return [self.f_ref[first + c, here, :] - self.f_ref[first + c, following, :] for c in range(5)]

    def mean_change(self, j, c):
        return self.pair(5 + c, j) + self.pair(5 + c, j, 1)


def along_lanes(first_line, flag_ref, q_ref, out_ref, mark_ref, z_ref, t_ref, v_ref, p_ref, w_ref, f_ref, sems):
    size_x, size_y, width = q_ref.shape[1:]
    q_flat = q_ref.reshape(5, size_x * size_y, width)
    t_flat = t_ref.reshape(width // LANES, 5, LANES, LANES)
    mark_ref[...] = jnp.zeros_like(mark_ref)
    groups = width // LANES
    steps = width // ROWS
    blocks = flag_ref.shape[2]
    per_block = steps // blocks
    assert steps & (steps - 1) == 0 and blocks & (blocks - 1) == 0
    line = Line((v_ref, p_ref, w_ref, f_ref), 2, 1)

    def turn_in(g, carry):
        lanes = pl.ds(pl.multiple_of(g * LANES, LANES), LANES)
        for c in range(5):
            z_ref[c, lanes, :] = q_flat[c, pl.ds(first_line, LANES), lanes].T
        return carry

    def leave(g):
        return pltpu.make_async_copy(t_ref.at[g], out_ref.at[0, g], sems.at[g])

    def turn_out(g):
        lanes = pl.ds(pl.multiple_of(g * LANES, LANES), LANES)
        for c in range(5):
            t_flat[g, c] = z_ref[5 + c, lanes, :].T
        leave(g).start()

    def chunk_of(i):
        return (i + (steps - 2)) & (steps - 1)

    def fetch(i):
        at = chunk_of(i)
        rows = pl.ds(pl.multiple_of(at * ROWS, ROWS), ROWS)
        return [z_ref[c, rows, :] for c in range(5)]


    def flag_of(block):
        return flag_ref[0, 0, (block + blocks) & (blocks - 1)]

    def finish(j, flag):
        j = jnp.maximum(j, 0)
        at = jnp.maximum(j - 2, 0)
        rows = pl.ds(pl.multiple_of(at * ROWS, ROWS), ROWS)
        first = jnp.where(flag > 0, 5, 0)
        for c, value in enumerate(line.change(j, first)):
            z_ref[5 + c, rows, :] = value - line.mean_change(j, c)

    lax.fori_loop(0, groups, turn_in, 0, unroll=True)

    def lead(i, carry):
        line.cell(i, fetch(i))
        return carry

    lax.fori_loop(1, 3 + per_block, lead, 0)

    def body(block, carry):
        start = 2 + block * per_block
        own, one, two = flag_of(block), flag_of(block - 1), flag_of(block - 2)
        steps_here = [start + k for k in range(per_block)]

        def lagging():
            finish(start - per_block - 1, two)
            for i in steps_here[:-1]:
                finish(i - per_block, one)

        @pl.when(own + one + two > 0)
        def _():
            for i in steps_here:
                line.face(i - per_block)
            lagging()
            d_flux = [line.fluxes(i) for i in steps_here]
            for i, d in zip(steps_here, d_flux):
                line.waves(i, d)
            for i, d in zip(steps_here, d_flux):
                line.central(i, d)
            for i in steps_here:
                line.cell(i + per_block + 1, fetch(i + per_block + 1))

        @pl.when(own + one + two <= 0)
        def _():
            lagging()
            for i in steps_here:
                line.central(i, line.fluxes(i))
            for i in steps_here:
                line.cell(i + per_block + 1, fetch(i + per_block + 1))

        return carry

    per_group = blocks // groups

    def lane_group(g, carry):
        lax.fori_loop(g * per_group, (g + 1) * per_group, body, 0)

        @pl.when(g > 0)
        def _():
            turn_out(g - 1)

        return carry

    lax.fori_loop(0, groups, lane_group, 0)
    for k in range(per_block):
        line.face(steps + 2 - per_block + k)
    for c in range(10):
        f_ref[c, pl.ds(ROWS * (steps + 2), ROWS), :] = f_ref[c, pl.ds(2 * ROWS, ROWS), :]
    for i in range(steps + 1 - per_block, steps + 2):
        finish(i, flag_of((i - 2) // per_block))
    turn_out(groups - 1)
    for g in range(groups):
        leave(g).wait()


def along_others(
    flag_ref, top_ref, q_ref, xl_ref, xr_ref, yl_ref, yr_ref, za_ref, zb_ref, adv_ref, ten_ref, v_ref, p_ref, w_ref, f_ref, ty_ref
):
    group = pl.program_id(0)
    size_x, size_y = q_ref.shape[1], q_ref.shape[2]
    q_flat = q_ref.reshape(5, size_x * size_y, LANES)
    ty_flat = ty_ref.reshape(5, size_y * size_x, LANES)
    per_group = flag_ref.shape[2] // pl.num_programs(0)
    edge = LANES // per_group
    lane_block = lax.broadcasted_iota(jnp.int32, (ROWS, LANES), 1) // edge
    marks = jnp.zeros((ROWS, LANES), jnp.int32)
    some = jnp.int32(0)
    for b in range(per_group):
        flag = flag_ref[0, 0, group * per_group + b]
        marks = jnp.where(lane_block == b, flag, marks)
        some = jnp.maximum(some, flag)
    shock = marks > 0

    def march(normal, count, left, middle, right, store):
        line = Line((v_ref, p_ref, w_ref, f_ref), normal, ROWS)

        def from_left(i, carry):
            line.cell(1 + i, left(i))
            return carry

        def from_middle(i, carry):
            line.cell(4 + i, middle(i))
            return carry

        lax.fori_loop(0, 3, from_left, 0, unroll=True)
        lax.fori_loop(0, 4, from_middle, 0, unroll=True)

        def ahead(j):
            inner = j - 1 < count
            near = middle(jnp.minimum(j - 1, count - 1))
            far = right(jnp.clip(j - 1 - count, 0, 2))
            line.cell(j + 3, [jnp.where(inner, n, f) for n, f in zip(near, far)])

        def finish(j, sharp):
            at = jnp.maximum(j - 4, 0)
            change = line.change(j, 0)
            if sharp:
                change = [jnp.where(shock, w, c) for w, c in zip(line.change(j, 5), change)]
            for c in range(5):
                store(at, c, change[c] - line.mean_change(j, c))

        @pl.when(some > 0)
        def _():
            def waves(steps):
                d_flux = [line.fluxes(j) for j in steps]
                for j, d in zip(steps, d_flux):
                    line.waves(j, d)
                for j, d in zip(steps, d_flux):
                    line.central(j, d)

            def two(n, carry):
                j = 4 + 2 * n
                for k in (2, 1):
                    line.face(j - k)
                for k in (3, 2):
                    finish(j - k, True)
                waves([j, j + 1])
                for k in (1, 2):
                    ahead(j + k)
                return carry

            pairs = (count + 1) // 2
            lax.fori_loop(0, pairs, two, 0)
            left_over = list(range(4 + 2 * pairs, 5 + count))
            waves(left_over)
            for j in [2 + 2 * pairs, 3 + 2 * pairs] + left_over:
                line.face(j)
            for j in range(1 + 2 * pairs, 4 + count):
                finish(j, True)

        @pl.when(some <= 0)
        def _():
            def body(j, carry):
                ahead(j)
                line.central(j, line.fluxes(j))
                finish(j - 1, False)
                return carry

            lax.fori_loop(4, 5 + count, body, 0)

    def line_x(t, carry):
        rows = pl.ds(pl.multiple_of(t * ROWS, ROWS), ROWS)

        def store(at, c, value):
            ten_ref[c, at, rows, :] = value

        march(
            0,
            size_x,
            lambda i: [xl_ref[c, i, rows, :] for c in range(5)],
            lambda i: [q_ref[c, i, rows, :] for c in range(5)],
            lambda i: [xr_ref[c, i, rows, :] for c in range(5)],
            store,
        )
        return carry

    def line_y(t, carry):
        rows = pl.ds(pl.multiple_of(t * ROWS, ROWS), ROWS)

        def store(at, c, value):
            ty_ref[c, at, rows, :] = value

        march(
            1,
            size_y,
            lambda i: [yl_ref[c, i, rows, :] for c in range(5)],
            lambda i: [q_flat[c, pl.ds(t * (ROWS * size_y) + i, ROWS, stride=size_y), :] for c in range(5)],
            lambda i: [yr_ref[c, i, rows, :] for c in range(5)],
            store,
        )
        return carry

    lax.fori_loop(0, size_y // ROWS, line_x, 0)
    lax.fori_loop(0, size_x // ROWS, line_y, 0)
    step = COURANT / jnp.max(top_ref[...], axis=0, keepdims=True)
    half = size_x // 2

    def last(x, carry):
        for h, part_ref in enumerate((za_ref, zb_ref)):
            for t in range(size_y // ROWS):
                rows = pl.ds(t * ROWS, ROWS)
                for c in range(5):
                    at = h * half + x
                    other = ty_flat[c, pl.ds(t * (ROWS * size_x) + at, ROWS, stride=size_x), :]
                    total = ten_ref[c, at, rows, :] + other + part_ref[c, x, rows, :]
                    ten_ref[c, at, rows, :] = total
                    adv_ref[c, at, rows, :] = q_ref[c, at, rows, :] + step * total
        return carry

    lax.fori_loop(0, half, last, 0)


def prepare(q_ref, xf_ref, xl_ref, yf_ref, yl_ref, top_ref):
    size_x, size_y, width = q_ref.shape[1:]

    def speeds(x, top):
        for t in range(size_y // ROWS):
            for g in range(width // LANES):
                q = [q_ref[c, x, pl.ds(t * ROWS, ROWS), pl.ds(g * LANES, LANES)] for c in range(5)]
                inv = 1.0 / q[0]
                kinetic = 0.5 * (q[1] * q[1] + q[2] * q[2] + q[3] * q[3]) * inv
                sound_sq = (GAMMA * GAMMA_LESS) * (q[4] - kinetic) * inv
                sound = sound_sq * lax.rsqrt(jnp.maximum(sound_sq, TINY))
                total = (jnp.abs(q[1]) + jnp.abs(q[2]) + jnp.abs(q[3])) * inv + 3.0 * sound
                top = jnp.maximum(top, total)
        for c in range(5):
            for k in range(3):
                yf_ref[c, k, pl.ds(x, 1), :] = q_ref[c, x, pl.ds(k, 1), :]
                yl_ref[c, k, pl.ds(x, 1), :] = q_ref[c, x, pl.ds(size_y - 3 + k, 1), :]
        return top

    top = lax.fori_loop(0, size_x, speeds, jnp.zeros((ROWS, LANES), jnp.float32))
    top_ref[...] = jnp.full(top_ref.shape, jnp.max(top), jnp.float32)
    for c in range(5):
        for k in range(3):
            xf_ref[c, k] = q_ref[c, k]
            xl_ref[c, k] = q_ref[c, size_x - 3 + k]


def line_scratch(rows):
    return [pltpu.VMEM((count, rows, LANES), jnp.float32) for count in (15, 19, 10, 10)]


WHOLE = pl.BlockSpec(memory_space=pltpu.VMEM)
SPARE = 28


def call_prepare(conserved, rows):
    _, size_x, size_y, size_z = conserved.shape
    layers = jax.ShapeDtypeStruct((5, 3, size_y, size_z), jnp.float32)
    turned = jax.ShapeDtypeStruct((5, 3, size_x, size_z), jnp.float32)
    return pl.pallas_call(
        prepare,
        out_shape=[layers, layers, turned, turned, jax.ShapeDtypeStruct((rows, LANES), jnp.float32)],
        in_specs=[WHOLE],
        out_specs=[WHOLE] * 5,
        cost_estimate=pl.CostEstimate(flops=4_000_000, bytes_accessed=2 * conserved.size * 4, transcendentals=0),
        compiler_params=pltpu.CompilerParams(vmem_limit_bytes=12 << 20),
        name="prepare",
    )(conserved)


def call_lanes(flags, conserved, part):
    _, size_x, size_y, size_z = conserved.shape
    block = (size_z // LANES, 5, LANES // size_y, size_y, LANES)
    return pl.pallas_call(
        functools.partial(along_lanes, part * LANES),
        out_shape=[jax.ShapeDtypeStruct((SPARE, *block), jnp.float32), jax.ShapeDtypeStruct((ROWS, LANES), jnp.float32)],
        in_specs=[pl.BlockSpec(memory_space=pltpu.SMEM), WHOLE],
        out_specs=[pl.BlockSpec(memory_space=pl.ANY), WHOLE],
        scratch_shapes=[pltpu.VMEM((10, size_z, LANES), jnp.float32), pltpu.VMEM(block, jnp.float32)]
        + line_scratch(size_z + 8 * ROWS)
        + [pltpu.SemaphoreType.DMA((size_z // LANES,))],
        cost_estimate=pl.CostEstimate(flops=60_000_000, bytes_accessed=conserved.size * 4, transcendentals=0),
        compiler_params=pltpu.CompilerParams(vmem_limit_bytes=30 << 20),
        name="along_lanes",
    )(flags, conserved)


def call_others(flags, top, conserved, x_low, x_high, y_low, y_high, parts):
    _, size_x, size_y, size_z = conserved.shape

    def spec(first, second):
        return pl.BlockSpec((5, first, second, LANES), lambda g: (0, 0, 0, g))

    whole = spec(size_x, size_y)
    part = pl.BlockSpec((pl.Squeezed(), pl.Squeezed(), 5, size_x // 2, size_y, LANES), lambda g: (0, g, 0, 0, 0, 0))
    return pl.pallas_call(
        along_others,
        out_shape=[jax.ShapeDtypeStruct(conserved.shape, jnp.float32)] * 2,
        grid=(size_z // LANES,),
        in_specs=[
            pl.BlockSpec(memory_space=pltpu.SMEM),
            pl.BlockSpec(top.shape, lambda g: (0, 0)),
            whole,
            spec(3, size_y),
            spec(3, size_y),
            spec(3, size_x),
            spec(3, size_x),
            part,
            part,
        ],
        out_specs=[whole, whole],
        scratch_shapes=line_scratch((max(size_x, size_y) + 9) * ROWS)
        + [pltpu.VMEM((5, size_y, size_x, LANES), jnp.float32)],
        cost_estimate=pl.CostEstimate(flops=240_000_000, bytes_accessed=4 * conserved.size * 4, transcendentals=0),
        compiler_params=pltpu.CompilerParams(vmem_limit_bytes=24 << 20),
        name="along_others",
    )(flags, top, conserved, x_low, x_high, y_low, y_high, *parts)


GX = ("ga", "gb")
SPLIT = 4


def neighbours(axis, first, last):
    size = lax.axis_size(axis)
    up = [(i, (i + 1) % size) for i in range(size)]
    down = [(j, i) for i, j in up]
    return lax.ppermute(last, axis, up), lax.ppermute(first, axis, down)


def swap(rows, axes):
    return lax.all_to_all(rows, axes, 0, 0, tiled=True)


def shards(conserved, shock_flags):
    inner, outer = ("gb",), ("ga", "gy")
    count, others = lax.axis_size(inner), lax.axis_size(outer)
    x_first, x_last, y_first, y_last, top = call_prepare(conserved, count)
    x_low, x_high = neighbours(GX, x_first, x_last)
    y_low, y_high = neighbours("gy", y_first, y_last)
    top = swap(top, inner)
    first, mark = call_lanes(shock_flags, conserved, 0)
    top = jnp.maximum(jnp.max(top, axis=0, keepdims=True), mark[:1])
    top = swap(jnp.broadcast_to(top, (others, LANES)), outer)
    second, _ = call_lanes(shock_flags, conserved, 1)
    return call_others(shock_flags, top, conserved, x_low, x_high, y_low, y_high, (first, second))


def local(conserved, shock_flags, top, x_low, x_high, y_low, y_high):
    x_first, x_last, y_first, y_last, mine = call_prepare(conserved, 16)
    parts = [call_lanes(shock_flags, conserved, h)[0] for h in range(2)]
    return call_others(shock_flags, mine, conserved, x_last, x_first, y_last, y_first, parts)


def solution(mesh):
    devices = mesh.devices
    size_x, size_y = devices.shape
    mesh = jax.sharding.Mesh(devices.reshape(SPLIT, size_x // SPLIT, size_y), (*GX, "gy"))
    spec = P(None, GX, "gy", None)
    return jax.shard_map(
        shards,
        mesh=mesh,
        in_specs=(spec, P(GX, "gy", None)),
        out_specs=(spec, spec),
        check_vma=False,
    )
```

profile of v0, /device:TPU:7, one launch (start us, length us, event | category | flops | bytes accessed | tf_op | source)
XLA Modules:
  0.0 84.7 jit_solution(4773989680863945718)
XLA Ops:
  0.6 0.0 copy-start
  0.6 1.7 %copy-done = f32[5,16,16,512]{3,2,1,0:T(8,128)S(1)} copy-done((f32[5,16,16,512]{3,2,1,0:T(8,128)S(1)}, f32[5,16,16,512]{3,2,1,0:T(8,128)}, u32[]{:S(2)}) %copy-start) | copy-done | bytes 2621464
  2.4 0.0 copy-start.1
  2.4 0.0 copy-start.2
  2.4 2.0 %prepare.1 = (f32[5,3,16,512]{3,2,1,0:T(8,128)}, f32[5,3,16,512]{3,2,1,0:T(8,128)}, f32[5,3,16,512]{3,2,1,0:T(8,128)}, f32[5,3,16,512]{3,2,1,0:T(8,128)}, f32[16,128]{1,0:T(8,128)}) custom-call(f32[5,16,16,512]{3,2,1,0:T(8,128)S(1)} %copy-done), custom_call_target="tpu_custom_call" | custom-call | flops 4000000 | bytes 5242880 | tf_op jit(solution)/shard_map/prepare/pallas_call | solution.py:475
  4.4 2.1 %collective-permute-start = (f32[5,3,16,512]{3,2,1,0:T(8,128)}, f32[5,3,16,512]{3,2,1,0:T(8,128)S(1)}, u32[]{:S(2)}, u32[]{:S(2)}) collective-permute-start(f32[5,3,16,512]{3,2,1,0:T(8,128)} %get-tuple-element.12), channel_id=1, source_target_pairs={{0,4},{4,8},{8,12},{12,16},{16,20},{20,24},{24,28},{28,32},{32,36}... | collective-permute-start | bytes 1474568 | tf_op jit(solution)/shard_map/ppermute | solution.py:543
  6.5 0.0 collective-permute-start.1
  6.5 1.3 %collective-permute-start.2 = (f32[5,3,16,512]{3,2,1,0:T(8,128)}, f32[5,3,16,512]{3,2,1,0:T(8,128)}, u32[]{:S(2)}, u32[]{:S(2)}) collective-permute-start(f32[5,3,16,512]{3,2,1,0:T(8,128)} %get-tuple-element.14), channel_id=1, source_target_pairs={{0,1},{1,2},{2,3},{3,0},{4,5},{5,6},{6,7},{7,4},{8,9},{9,10},{10,1... | collective-permute-start | bytes 1474568 | tf_op jit(solution)/shard_map/ppermute | solution.py:543
  7.8 1.4 %collective-permute-start.3 = (f32[5,3,16,512]{3,2,1,0:T(8,128)}, f32[5,3,16,512]{3,2,1,0:T(8,128)}, u32[]{:S(2)}, u32[]{:S(2)}) collective-permute-start(f32[5,3,16,512]{3,2,1,0:T(8,128)} %get-tuple-element.15), channel_id=1, source_target_pairs={{1,0},{2,1},{3,2},{0,3},{5,4},{6,5},{7,6},{4,7},{9,8},{10,9},{11,1... | collective-permute-start | bytes 1474568 | tf_op jit(solution)/shard_map/ppermute | solution.py:543
  9.2 9.9 %all-to-all-start = ((f32[16,1,128]{2,1,0:T(1,128)}), f32[16,1,128]{2,1,0:T(1,128)S(1)}, u32[]{:S(2)}, u32[]{:S(2)}) async-start(f32[16,1,128]{2,1,0:T(1,128)} %bitcast.1), calls=%async_computation | async-start | bytes 16384 | tf_op jit(solution)/shard_map/all_to_all | solution.py:547
  19.1 0.0 copy-done.1
  19.1 0.0 copy-done.2
  19.1 10.9 %along_lanes.2 = (f32[28,4,5,8,16,128]{5,4,3,2,1,0:T(8,128)}, f32[8,128]{1,0:T(8,128)S(1)}) custom-call(s32[1,1,32]{2,1,0:T(1,128)S(1)} %copy-done.2, f32[5,16,16,512]{3,2,1,0:T(8,128)S(1)} %copy-done.1), custom_call_target="tpu_custom_call" | custom-call | flops 60000000 | bytes 2621440 | tf_op jit(solution)/shard_map/along_lanes/pallas_call | solution.py:489
  30.0 0.0 all-to-all-done
  30.0 0.6 broadcast_in_dim.9
  30.6 5.5 %all-to-all-start.1 = ((f32[16,1,128]{2,1,0:T(1,128)}), f32[16,1,128]{2,1,0:T(1,128)S(1)}, u32[]{:S(2)}, u32[]{:S(2)}) async-start(f32[16,1,128]{2,1,0:T(1,128)} %broadcast_in_dim.9), calls=%async_computation.1 | async-start | bytes 16384 | tf_op jit(solution)/shard_map/all_to_all | solution.py:547
  36.1 11.5 %along_lanes.3 = (f32[28,4,5,8,16,128]{5,4,3,2,1,0:T(8,128)}, f32[8,128]{1,0:T(8,128)}) custom-call(s32[1,1,32]{2,1,0:T(1,128)S(1)} %copy-done.2, f32[5,16,16,512]{3,2,1,0:T(8,128)S(1)} %copy-done.1), custom_call_target="tpu_custom_call" | custom-call | flops 60000000 | bytes 2621440 | tf_op jit(solution)/shard_map/along_lanes/pallas_call | solution.py:489
  47.6 0.0 all-to-all-done.1
  47.6 0.0 collective-permute-done.xl_ref
  47.6 0.0 collective-permute-done.1.xr_ref
  47.6 0.0 collective-permute-done.2.yl_ref
  47.7 0.0 collective-permute-done.3.yr_ref
  47.7 37.0 %along_others.1 = (f32[5,16,16,512]{3,2,1,0:T(8,128)}, f32[5,16,16,512]{3,2,1,0:T(8,128)}) custom-call(s32[1,1,32]{2,1,0:T(1,128)S(1)} %copy-done.2, f32[16,128]{1,0:T(8,128)S(1)} %bitcast.10, f32[5,16,16,512]{3,2,1,0:T(8,128)S(1)} %copy-done.1, f32[5,3,16,512]{3,2,1,0:T(8,128)S(1)} %collective-permute-done.xl_ref, ...), custom_call_target="tpu_custom_call" | custom-call | flops 240000000 | bytes 10485760 | tf_op jit(solution)/shard_map/along_others/pallas_call | solution.py:511
  (2 shorter events, 0.0 us)
Async XLA Ops:
  0.6 1.7 %copy-start = (f32[5,16,16,512]{3,2,1,0:T(8,128)S(1)}, f32[5,16,16,512]{3,2,1,0:T(8,128)}, u32[]{:S(2)}) copy-start(f32[5,16,16,512]{3,2,1,0:T(8,128)} %q_ref.7) | copy-start | bytes 7864324
  2.4 16.7 %copy-start.1 = (f32[5,16,16,512]{3,2,1,0:T(8,128)S(1)}, f32[5,16,16,512]{3,2,1,0:T(8,128)}, u32[]{:S(2)}) copy-start(f32[5,16,16,512]{3,2,1,0:T(8,128)} %q_ref.7) | copy-start | bytes 7864324
  2.4 16.7 %copy-start.2 = (s32[1,1,32]{2,1,0:T(1,128)S(1)}, s32[1,1,32]{2,1,0:T(1,128)}, u32[]{:S(2)}) copy-start(s32[1,1,32]{2,1,0:T(1,128)} %flag_ref.5) | copy-start | bytes 388
  4.4 43.3 %collective-permute-start = (f32[5,3,16,512]{3,2,1,0:T(8,128)}, f32[5,3,16,512]{3,2,1,0:T(8,128)S(1)}, u32[]{:S(2)}, u32[]{:S(2)}) collective-permute-start(f32[5,3,16,512]{3,2,1,0:T(8,128)} %get-tuple-element.12), channel_id=1, source_target_pairs={{0,4},{4,8},{8,12},{12,16},{16,20},{20,24},{24,28},{28,32},{32,36}... | collective-permute-start | bytes 1474568 | tf_op jit(solution)/shard_map/ppermute | solution.py:543
  6.5 41.2 %collective-permute-start.1 = (f32[5,3,16,512]{3,2,1,0:T(8,128)}, f32[5,3,16,512]{3,2,1,0:T(8,128)}, u32[]{:S(2)}, u32[]{:S(2)}) collective-permute-start(f32[5,3,16,512]{3,2,1,0:T(8,128)} %get-tuple-element.13), channel_id=1, source_target_pairs={{4,0},{8,4},{12,8},{16,12},{20,16},{24,20},{28,24},{32,28},{36,32}... | collective-permute-start | bytes 1474568 | tf_op jit(solution)/shard_map/ppermute | solution.py:543
  6.5 41.2 %collective-permute-start.2 = (f32[5,3,16,512]{3,2,1,0:T(8,128)}, f32[5,3,16,512]{3,2,1,0:T(8,128)}, u32[]{:S(2)}, u32[]{:S(2)}) collective-permute-start(f32[5,3,16,512]{3,2,1,0:T(8,128)} %get-tuple-element.14), channel_id=1, source_target_pairs={{0,1},{1,2},{2,3},{3,0},{4,5},{5,6},{6,7},{7,4},{8,9},{9,10},{10,1... | collective-permute-start | bytes 1474568 | tf_op jit(solution)/shard_map/ppermute | solution.py:543
  7.8 39.9 %collective-permute-start.3 = (f32[5,3,16,512]{3,2,1,0:T(8,128)}, f32[5,3,16,512]{3,2,1,0:T(8,128)}, u32[]{:S(2)}, u32[]{:S(2)}) collective-permute-start(f32[5,3,16,512]{3,2,1,0:T(8,128)} %get-tuple-element.15), channel_id=1, source_target_pairs={{1,0},{2,1},{3,2},{0,3},{5,4},{6,5},{7,6},{4,7},{9,8},{10,9},{11,1... | collective-permute-start | bytes 1474568 | tf_op jit(solution)/shard_map/ppermute | solution.py:543
  9.2 20.8 %all-to-all-start = ((f32[16,1,128]{2,1,0:T(1,128)}), f32[16,1,128]{2,1,0:T(1,128)S(1)}, u32[]{:S(2)}, u32[]{:S(2)}) async-start(f32[16,1,128]{2,1,0:T(1,128)} %bitcast.1), calls=%async_computation | async-start | bytes 16384 | tf_op jit(solution)/shard_map/all_to_all | solution.py:547
  30.6 17.0 %all-to-all-start.1 = ((f32[16,1,128]{2,1,0:T(1,128)}), f32[16,1,128]{2,1,0:T(1,128)S(1)}, u32[]{:S(2)}, u32[]{:S(2)}) async-start(f32[16,1,128]{2,1,0:T(1,128)} %broadcast_in_dim.9), calls=%async_computation.1 | async-start | bytes 16384 | tf_op jit(solution)/shard_map/all_to_all | solution.py:547
where the time goes:
time: 86.2 us; the launch traced here: 84.7 us
  Pallas kernels  61.3 us (71%)
  starting transfers between devices  20.2 us (23%)
  local copies, waits for them, and re-layouts  2.34 us (3%)
    pallas_call x1, Pallas kernels, call_others(): pl.pallas_call(along_others, out_shape=[jax.ShapeDtypeStruct(conserved.sh...  37 us
    pallas_call x2, Pallas kernels, call_lanes(): pl.pallas_call(functools.partial(along_lanes, part * LANES), out_shape=[j...  22.3 us
    all_to_all x2, starting transfers between devices, swap(): return lax.all_to_all(rows, axes, 0, 0, tiled=True)  15.4 us
    ppermute x4, starting transfers between devices, neighbours(): return (lax.ppermute(last, axis, up), lax.ppermute(first, axis, down))  4.85 us
    pallas_call x1, Pallas kernels, call_prepare(): pl.pallas_call(prepare, out_shape=[layers, layers, turned, turned, jax.Sh...  1.98 us
    unnamed x6, local copies, waits for them, and re-layouts  1.74 us
  transfers between devices with their start and end apart: 6, of which 0 were waited for; matrix products, arithmetic and copies ran while one was open for 1% of the time, Pallas kernels for 26%

commit v1 on v0

--- a/solution.py
+++ b/solution.py
@@ -185,11 +185,11 @@
         return self.pair(5 + c, j) + self.pair(5 + c, j, 1)
 
 
-def along_lanes(first_line, flag_ref, q_ref, out_ref, mark_ref, z_ref, t_ref, v_ref, p_ref, w_ref, f_ref, sems):
+def along_lanes(flag_ref, q_ref, out_ref, z_ref, t_ref, v_ref, p_ref, w_ref, f_ref, sems):
     size_x, size_y, width = q_ref.shape[1:]
     q_flat = q_ref.reshape(5, size_x * size_y, width)
-    t_flat = t_ref.reshape(width // LANES, 5, LANES, LANES)
-    mark_ref[...] = jnp.zeros_like(mark_ref)
+    parts = size_x * size_y // LANES
+    t_flat = t_ref.reshape(parts * (width // LANES), 5, LANES, LANES)
     groups = width // LANES
     steps = width // ROWS
     blocks = flag_ref.shape[2]
@@ -197,20 +197,21 @@
     assert steps & (steps - 1) == 0 and blocks & (blocks - 1) == 0
     line = Line((v_ref, p_ref, w_ref, f_ref), 2, 1)
 
-    def turn_in(g, carry):
+    def turn_in(part, g):
+        lines = pl.ds(pl.multiple_of(part * LANES, LANES), LANES)
         lanes = pl.ds(pl.multiple_of(g * LANES, LANES), LANES)
         for c in range(5):
-            z_ref[c, lanes, :] = q_flat[c, pl.ds(first_line, LANES), lanes].T
-        return carry
-
-    def leave(g):
-        return pltpu.make_async_copy(t_ref.at[g], out_ref.at[0, g], sems.at[g])
-
-    def turn_out(g):
+            z_ref[c, lanes, :] = q_flat[c, lines, lanes].T
+
+    def leave(slot):
+        return pltpu.make_async_copy(t_ref.at[slot], out_ref.at[0, slot], sems.at[slot])
+
+    def turn_out(part, g):
         lanes = pl.ds(pl.multiple_of(g * LANES, LANES), LANES)
+        slot = part * groups + g
         for c in range(5):
-            t_flat[g, c] = z_ref[5 + c, lanes, :].T
-        leave(g).start()
+            t_flat[slot, c] = z_ref[5 + c, lanes, :].T
+        leave(slot).start()
 
     def chunk_of(i):
         return (i + (steps - 2)) & (steps - 1)
@@ -232,13 +233,9 @@
         for c, value in enumerate(line.change(j, first)):
             z_ref[5 + c, rows, :] = value - line.mean_change(j, c)
 
-    lax.fori_loop(0, groups, turn_in, 0, unroll=True)
-
     def lead(i, carry):
         line.cell(i, fetch(i))
         return carry
-
-    lax.fori_loop(1, 3 + per_block, lead, 0)
 
     def body(block, carry):
         start = 2 + block * per_block
@@ -275,25 +272,33 @@
 
     per_group = blocks // groups
 
-    def lane_group(g, carry):
-        lax.fori_loop(g * per_group, (g + 1) * per_group, body, 0)
-
-        @pl.when(g > 0)
-        def _():
-            turn_out(g - 1)
-
+    def one_part(part, carry):
+        for g in range(groups):
+            turn_in(part, g)
+        lax.fori_loop(1, 3 + per_block, lead, 0)
+
+        def lane_group(g, carry):
+            lax.fori_loop(g * per_group, (g + 1) * per_group, body, 0)
+
+            @pl.when(g > 0)
+            def _():
+                turn_out(part, g - 1)
+
+            return carry
+
+        lax.fori_loop(0, groups, lane_group, 0)
+        for k in range(per_block):
+            line.face(steps + 2 - per_block + k)
+        for c in range(10):
+            f_ref[c, pl.ds(ROWS * (steps + 2), ROWS), :] = f_ref[c, pl.ds(2 * ROWS, ROWS), :]
+        for i in range(steps + 1 - per_block, steps + 2):
+            finish(i, flag_of((i - 2) // per_block))
+        turn_out(part, groups - 1)
         return carry
 
-    lax.fori_loop(0, groups, lane_group, 0)
-    for k in range(per_block):
-        line.face(steps + 2 - per_block + k)
-    for c in range(10):
-        f_ref[c, pl.ds(ROWS * (steps + 2), ROWS), :] = f_ref[c, pl.ds(2 * ROWS, ROWS), :]
-    for i in range(steps + 1 - per_block, steps + 2):
-        finish(i, flag_of((i - 2) // per_block))
-    turn_out(groups - 1)
-    for g in range(groups):
-        leave(g).wait()
+    lax.fori_loop(0, parts, one_part, 0)
+    for slot in range(parts * groups):
+        leave(slot).wait()
 
 
 def along_others(
@@ -465,7 +470,7 @@
 
 
 WHOLE = pl.BlockSpec(memory_space=pltpu.VMEM)
-SPARE = 28
+SPARE = 14
 
 
 def call_prepare(conserved, rows):
@@ -483,31 +488,37 @@
     )(conserved)
 
 
-def call_lanes(flags, conserved, part):
+def call_lanes(flags, conserved):
     _, size_x, size_y, size_z = conserved.shape
-    block = (size_z // LANES, 5, LANES // size_y, size_y, LANES)
+    parts = size_x * size_y // LANES
+    block = (parts * (size_z // LANES), 5, LANES // size_y, size_y, LANES)
     return pl.pallas_call(
-        functools.partial(along_lanes, part * LANES),
-        out_shape=[jax.ShapeDtypeStruct((SPARE, *block), jnp.float32), jax.ShapeDtypeStruct((ROWS, LANES), jnp.float32)],
+        along_lanes,
+        out_shape=jax.ShapeDtypeStruct((SPARE, *block), jnp.float32),
         in_specs=[pl.BlockSpec(memory_space=pltpu.SMEM), WHOLE],
-        out_specs=[pl.BlockSpec(memory_space=pl.ANY), WHOLE],
+        out_specs=pl.BlockSpec(memory_space=pl.ANY),
         scratch_shapes=[pltpu.VMEM((10, size_z, LANES), jnp.float32), pltpu.VMEM(block, jnp.float32)]
         + line_scratch(size_z + 8 * ROWS)
-        + [pltpu.SemaphoreType.DMA((size_z // LANES,))],
-        cost_estimate=pl.CostEstimate(flops=60_000_000, bytes_accessed=conserved.size * 4, transcendentals=0),
+        + [pltpu.SemaphoreType.DMA((block[0],))],
+        cost_estimate=pl.CostEstimate(flops=120_000_000, bytes_accessed=2 * conserved.size * 4, transcendentals=0),
         compiler_params=pltpu.CompilerParams(vmem_limit_bytes=30 << 20),
         name="along_lanes",
     )(flags, conserved)
 
 
-def call_others(flags, top, conserved, x_low, x_high, y_low, y_high, parts):
+def call_others(flags, top, conserved, x_low, x_high, y_low, y_high, part):
     _, size_x, size_y, size_z = conserved.shape
 
     def spec(first, second):
         return pl.BlockSpec((5, first, second, LANES), lambda g: (0, 0, 0, g))
 
     whole = spec(size_x, size_y)
-    part = pl.BlockSpec((pl.Squeezed(), pl.Squeezed(), 5, size_x // 2, size_y, LANES), lambda g: (0, g, 0, 0, 0, 0))
+    groups = size_z // LANES
+
+    def half(h):
+        block = (pl.Squeezed(), pl.Squeezed(), 5, size_x // 2, size_y, LANES)
+        return pl.BlockSpec(block, lambda g: (0, h * groups + g, 0, 0, 0, 0))
+
     return pl.pallas_call(
         along_others,
         out_shape=[jax.ShapeDtypeStruct(conserved.shape, jnp.float32)] * 2,
@@ -520,8 +531,8 @@
             spec(3, size_y),
             spec(3, size_x),
             spec(3, size_x),
-            part,
-            part,
+            half(0),
+            half(1),
         ],
         out_specs=[whole, whole],
         scratch_shapes=line_scratch((max(size_x, size_y) + 9) * ROWS)
@@ -529,11 +540,7 @@
         cost_estimate=pl.CostEstimate(flops=240_000_000, bytes_accessed=4 * conserved.size * 4, transcendentals=0),
         compiler_params=pltpu.CompilerParams(vmem_limit_bytes=24 << 20),
         name="along_others",
-    )(flags, top, conserved, x_low, x_high, y_low, y_high, *parts)
-
-
-GX = ("ga", "gb")
-SPLIT = 4
+    )(flags, top, conserved, x_low, x_high, y_low, y_high, part, part)
 
 
 def neighbours(axis, first, last):
@@ -543,39 +550,28 @@
     return lax.ppermute(last, axis, up), lax.ppermute(first, axis, down)
 
 
-def swap(rows, axes):
-    return lax.all_to_all(rows, axes, 0, 0, tiled=True)
-
-
 def shards(conserved, shock_flags):
-    inner, outer = ("gb",), ("ga", "gy")
-    count, others = lax.axis_size(inner), lax.axis_size(outer)
-    x_first, x_last, y_first, y_last, top = call_prepare(conserved, count)
-    x_low, x_high = neighbours(GX, x_first, x_last)
+    everyone = ("gx", "gy")
+    x_first, x_last, y_first, y_last, top = call_prepare(conserved, lax.axis_size(everyone))
+    x_low, x_high = neighbours("gx", x_first, x_last)
     y_low, y_high = neighbours("gy", y_first, y_last)
-    top = swap(top, inner)
-    first, mark = call_lanes(shock_flags, conserved, 0)
-    top = jnp.maximum(jnp.max(top, axis=0, keepdims=True), mark[:1])
-    top = swap(jnp.broadcast_to(top, (others, LANES)), outer)
-    second, _ = call_lanes(shock_flags, conserved, 1)
-    return call_others(shock_flags, top, conserved, x_low, x_high, y_low, y_high, (first, second))
+    top = lax.all_to_all(top, everyone, 0, 0, tiled=True)
+    part = call_lanes(shock_flags, conserved)
+    return call_others(shock_flags, top, conserved, x_low, x_high, y_low, y_high, part)
 
 
 def local(conserved, shock_flags, top, x_low, x_high, y_low, y_high):
-    x_first, x_last, y_first, y_last, mine = call_prepare(conserved, 16)
-    parts = [call_lanes(shock_flags, conserved, h)[0] for h in range(2)]
-    return call_others(shock_flags, mine, conserved, x_last, x_first, y_last, y_first, parts)
+    x_first, x_last, y_first, y_last, mine = call_prepare(conserved, 256)
+    part = call_lanes(shock_flags, conserved)
+    return call_others(shock_flags, mine, conserved, x_last, x_first, y_last, y_first, part)
 
 
 def solution(mesh):
-    devices = mesh.devices
-    size_x, size_y = devices.shape
-    mesh = jax.sharding.Mesh(devices.reshape(SPLIT, size_x // SPLIT, size_y), (*GX, "gy"))
-    spec = P(None, GX, "gy", None)
+    spec = P(None, "gx", "gy", None)
     return jax.shard_map(
         shards,
         mesh=mesh,
-        in_specs=(spec, P(GX, "gy", None)),
+        in_specs=(spec, P("gx", "gy", None)),
         out_specs=(spec, spec),
         check_vma=False,
     )

time: 86.2 us -> 81.7 us (0.948)
  the two profiles are of different devices: /device:TPU:7 before, /device:TPU:17 now
where the time goes in v1:
time: 81.7 us; the launch traced here: 81.4 us
  Pallas kernels  59.5 us (73%)
  starting transfers between devices  19.4 us (24%)
  local copies, waits for them, and re-layouts  1.74 us (2%)
    pallas_call x1, Pallas kernels, call_others(): pl.pallas_call(along_others, out_shape=[jax.ShapeDtypeStruct(conserved.sh...  37.1 us
    pallas_call x1, Pallas kernels, call_lanes(): pl.pallas_call(along_lanes, out_shape=jax.ShapeDtypeStruct((SPARE, *block...  20.5 us
    all_to_all x1, starting transfers between devices, shards(): top = lax.all_to_all(top, everyone, 0, 0, tiled=True)  16.2 us
    ppermute x4, starting transfers between devices, neighbours(): return (lax.ppermute(last, axis, up), lax.ppermute(first, axis, down))  3.24 us
    pallas_call x1, Pallas kernels, call_prepare(): pl.pallas_call(prepare, out_shape=[layers, layers, turned, turned, jax.Sh...  2 us
    unnamed x6, local copies, waits for them, and re-layouts  1.74 us
  transfers between devices with their start and end apart: 5, of which 0 were waited for; matrix products, arithmetic and copies ran while one was open for 0% of the time, Pallas kernels for 25%

profile of v1, /device:TPU:17, one launch (start us, length us, event | category | flops | bytes accessed | tf_op | source)
XLA Modules:
  0.0 81.4 jit_solution(16605380903061593903)
XLA Ops:
  0.6 0.0 copy-start
  0.6 1.7 %copy-done = f32[5,16,16,512]{3,2,1,0:T(8,128)S(1)} copy-done((f32[5,16,16,512]{3,2,1,0:T(8,128)S(1)}, f32[5,16,16,512]{3,2,1,0:T(8,128)}, u32[]{:S(2)}) %copy-start) | copy-done | bytes 2621464
  2.4 0.0 copy-start.1
  2.4 0.0 copy-start.2
  2.4 2.0 %prepare.1 = (f32[5,3,16,512]{3,2,1,0:T(8,128)}, f32[5,3,16,512]{3,2,1,0:T(8,128)}, f32[5,3,16,512]{3,2,1,0:T(8,128)}, f32[5,3,16,512]{3,2,1,0:T(8,128)}, f32[256,128]{1,0:T(8,128)}) custom-call(f32[5,16,16,512]{3,2,1,0:T(8,128)S(1)} %copy-done), custom_call_target="tpu_custom_call" | custom-call | flops 4000000 | bytes 5242880 | tf_op jit(solution)/shard_map/prepare/pallas_call | solution.py:480
  4.4 1.8 %collective-permute-start = (f32[5,3,16,512]{3,2,1,0:T(8,128)}, f32[5,3,16,512]{3,2,1,0:T(8,128)S(1)}, u32[]{:S(2)}, u32[]{:S(2)}) collective-permute-start(f32[5,3,16,512]{3,2,1,0:T(8,128)} %get-tuple-element.8), channel_id=1, source_target_pairs={{0,4},{4,8},{8,12},{12,16},{16,20},{20,24},{24,28},{28,32},{32,36}... | collective-permute-start | bytes 1474568 | tf_op jit(solution)/shard_map/ppermute | solution.py:550
  6.1 0.0 collective-permute-start.1
  6.2 1.0 %collective-permute-start.2 = (f32[5,3,16,512]{3,2,1,0:T(8,128)}, f32[5,3,16,512]{3,2,1,0:T(8,128)}, u32[]{:S(2)}, u32[]{:S(2)}) collective-permute-start(f32[5,3,16,512]{3,2,1,0:T(8,128)} %get-tuple-element.10), channel_id=1, source_target_pairs={{0,1},{1,2},{2,3},{3,0},{4,5},{5,6},{6,7},{7,4},{8,9},{9,10},{10,1... | collective-permute-start | bytes 1474568 | tf_op jit(solution)/shard_map/ppermute | solution.py:550
  7.2 0.5 collective-permute-start.3
  7.6 16.2 %all-to-all-start = ((f32[256,1,128]{2,1,0:T(1,128)}), f32[256,1,128]{2,1,0:T(1,128)S(1)}, u32[]{:S(2)}, u32[]{:S(2)}) async-start(f32[256,1,128]{2,1,0:T(1,128)} %bitcast.1), calls=%async_computation | async-start | bytes 262144 | tf_op jit(solution)/shard_map/all_to_all | solution.py:558
  23.8 0.0 copy-done.1
  23.8 0.0 copy-done.2
  23.8 20.5 %along_lanes.1.za_ref.zb_ref = f32[14,8,5,8,16,128]{5,4,3,2,1,0:T(8,128)} custom-call(s32[1,1,32]{2,1,0:T(1,128)S(1)} %copy-done.2, f32[5,16,16,512]{3,2,1,0:T(8,128)S(1)} %copy-done.1), custom_call_target="tpu_custom_call" | custom-call | flops 120000000 | bytes 5242880 | tf_op jit(solution)/shard_map/along_lanes/pallas_call | solution.py:495
  44.3 0.0 all-to-all-done
  44.3 0.0 collective-permute-done.xl_ref
  44.3 0.0 collective-permute-done.1.xr_ref
  44.3 0.0 collective-permute-done.2.yl_ref
  44.4 0.0 collective-permute-done.3.yr_ref
  44.4 37.1 %along_others.1 = (f32[5,16,16,512]{3,2,1,0:T(8,128)}, f32[5,16,16,512]{3,2,1,0:T(8,128)}) custom-call(s32[1,1,32]{2,1,0:T(1,128)S(1)} %copy-done.2, f32[256,128]{1,0:T(8,128)S(1)} %bitcast.4, f32[5,16,16,512]{3,2,1,0:T(8,128)S(1)} %copy-done.1, f32[5,3,16,512]{3,2,1,0:T(8,128)S(1)} %collective-permute-done.xl_ref, ...), custom_call_target="tpu_custom_call" | custom-call | flops 240000000 | bytes 10485760 | tf_op jit(solution)/shard_map/along_others/pallas_call | solution.py:522
Async XLA Ops:
  0.6 1.7 %copy-start = (f32[5,16,16,512]{3,2,1,0:T(8,128)S(1)}, f32[5,16,16,512]{3,2,1,0:T(8,128)}, u32[]{:S(2)}) copy-start(f32[5,16,16,512]{3,2,1,0:T(8,128)} %q_ref.5) | copy-start | bytes 7864324
  2.4 21.5 %copy-start.1 = (f32[5,16,16,512]{3,2,1,0:T(8,128)S(1)}, f32[5,16,16,512]{3,2,1,0:T(8,128)}, u32[]{:S(2)}) copy-start(f32[5,16,16,512]{3,2,1,0:T(8,128)} %q_ref.5) | copy-start | bytes 7864324
  2.4 21.5 %copy-start.2 = (s32[1,1,32]{2,1,0:T(1,128)S(1)}, s32[1,1,32]{2,1,0:T(1,128)}, u32[]{:S(2)}) copy-start(s32[1,1,32]{2,1,0:T(1,128)} %flag_ref.3) | copy-start | bytes 388
  4.4 40.0 %collective-permute-start = (f32[5,3,16,512]{3,2,1,0:T(8,128)}, f32[5,3,16,512]{3,2,1,0:T(8,128)S(1)}, u32[]{:S(2)}, u32[]{:S(2)}) collective-permute-start(f32[5,3,16,512]{3,2,1,0:T(8,128)} %get-tuple-element.8), channel_id=1, source_target_pairs={{0,4},{4,8},{8,12},{12,16},{16,20},{20,24},{24,28},{28,32},{32,36}... | collective-permute-start | bytes 1474568 | tf_op jit(solution)/shard_map/ppermute | solution.py:550
  6.1 38.2 %collective-permute-start.1 = (f32[5,3,16,512]{3,2,1,0:T(8,128)}, f32[5,3,16,512]{3,2,1,0:T(8,128)}, u32[]{:S(2)}, u32[]{:S(2)}) collective-permute-start(f32[5,3,16,512]{3,2,1,0:T(8,128)} %get-tuple-element.9), channel_id=1, source_target_pairs={{4,0},{8,4},{12,8},{16,12},{20,16},{24,20},{28,24},{32,28},{36,32}... | collective-permute-start | bytes 1474568 | tf_op jit(solution)/shard_map/ppermute | solution.py:550
  6.2 38.2 %collective-permute-start.2 = (f32[5,3,16,512]{3,2,1,0:T(8,128)}, f32[5,3,16,512]{3,2,1,0:T(8,128)}, u32[]{:S(2)}, u32[]{:S(2)}) collective-permute-start(f32[5,3,16,512]{3,2,1,0:T(8,128)} %get-tuple-element.10), channel_id=1, source_target_pairs={{0,1},{1,2},{2,3},{3,0},{4,5},{5,6},{6,7},{7,4},{8,9},{9,10},{10,1... | collective-permute-start | bytes 1474568 | tf_op jit(solution)/shard_map/ppermute | solution.py:550
  7.2 37.2 %collective-permute-start.3 = (f32[5,3,16,512]{3,2,1,0:T(8,128)}, f32[5,3,16,512]{3,2,1,0:T(8,128)}, u32[]{:S(2)}, u32[]{:S(2)}) collective-permute-start(f32[5,3,16,512]{3,2,1,0:T(8,128)} %get-tuple-element.11), channel_id=1, source_target_pairs={{1,0},{2,1},{3,2},{0,3},{5,4},{6,5},{7,6},{4,7},{9,8},{10,9},{11,1... | collective-permute-start | bytes 1474568 | tf_op jit(solution)/shard_map/ppermute | solution.py:550
  7.6 36.7 %all-to-all-start = ((f32[256,1,128]{2,1,0:T(1,128)}), f32[256,1,128]{2,1,0:T(1,128)S(1)}, u32[]{:S(2)}, u32[]{:S(2)}) async-start(f32[256,1,128]{2,1,0:T(1,128)} %bitcast.1), calls=%async_computation | async-start | bytes 262144 | tf_op jit(solution)/shard_map/all_to_all | solution.py:558

commit v2 on v1

--- a/solution.py
+++ b/solution.py
@@ -356,7 +356,7 @@
                 for j, d in zip(steps, d_flux):
                     line.central(j, d)
 
-            def two(n, carry):
+            def two(n, source):
                 j = 4 + 2 * n
                 for k in (2, 1):
                     line.face(j - k)
@@ -364,11 +364,12 @@
                     finish(j - k, True)
                 waves([j, j + 1])
                 for k in (1, 2):
-                    ahead(j + k)
-                return carry
+                    line.cell(j + k + 3, source(j + k - 1))
+                return 0
 
             pairs = (count + 1) // 2
-            lax.fori_loop(0, pairs, two, 0)
+            lax.fori_loop(0, pairs - 2, lambda n, _: two(n, middle), 0)
+            lax.fori_loop(pairs - 2, pairs, lambda n, _: two(n, lambda i: right(jnp.minimum(i - count, 2))), 0)
             left_over = list(range(4 + 2 * pairs, 5 + count))
             waves(left_over)
             for j in [2 + 2 * pairs, 3 + 2 * pairs] + left_over:
@@ -438,7 +439,7 @@
     lax.fori_loop(0, half, last, 0)
 
 
-def prepare(q_ref, xf_ref, xl_ref, yf_ref, yl_ref, top_ref):
+def prepare(from_ref, xf_ref, xl_ref, yf_ref, yl_ref, top_ref, q_ref, sems):
     size_x, size_y, width = q_ref.shape[1:]
 
     def speeds(x, top):
@@ -457,7 +458,19 @@
                 yl_ref[c, k, pl.ds(x, 1), :] = q_ref[c, x, pl.ds(size_y - 3 + k, 1), :]
         return top
 
-    top = lax.fori_loop(0, size_x, speeds, jnp.zeros((ROWS, LANES), jnp.float32))
+    chunks = sems.shape[0]
+    per_chunk = size_x // chunks
+
+    def enter(i):
+        rows = pl.ds(i * per_chunk, per_chunk)
+        return pltpu.make_async_copy(from_ref.at[:, rows], q_ref.at[:, rows], sems.at[i])
+
+    for i in range(chunks):
+        enter(i).start()
+    top = jnp.zeros((ROWS, LANES), jnp.float32)
+    for i in range(chunks):
+        enter(i).wait()
+        top = lax.fori_loop(i * per_chunk, (i + 1) * per_chunk, speeds, top)
     top_ref[...] = jnp.full(top_ref.shape, jnp.max(top), jnp.float32)
     for c in range(5):
         for k in range(3):
@@ -480,10 +493,10 @@
     return pl.pallas_call(
         prepare,
         out_shape=[layers, layers, turned, turned, jax.ShapeDtypeStruct((rows, LANES), jnp.float32)],
-        in_specs=[WHOLE],
+        in_specs=[pl.BlockSpec(memory_space=pl.ANY)],
         out_specs=[WHOLE] * 5,
+        scratch_shapes=[pltpu.VMEM(conserved.shape, jnp.float32), pltpu.SemaphoreType.DMA((4,))],
         cost_estimate=pl.CostEstimate(flops=4_000_000, bytes_accessed=2 * conserved.size * 4, transcendentals=0),
-        compiler_params=pltpu.CompilerParams(vmem_limit_bytes=12 << 20),
         name="prepare",
     )(conserved)
 

time: 81.7 us -> 79.9 us (0.978)
  the two profiles are of different devices: /device:TPU:17 before, /device:TPU:131 now
where the time goes in v2:
time: 79.9 us; the launch traced here: 79.3 us
  Pallas kernels  59.7 us (75%)
  starting transfers between devices  18.8 us (24%)
    pallas_call x1, Pallas kernels, call_others(): pl.pallas_call(along_others, out_shape=[jax.ShapeDtypeStruct(conserved.sh...  35.9 us
    pallas_call x1, Pallas kernels, call_lanes(): pl.pallas_call(along_lanes, out_shape=jax.ShapeDtypeStruct((SPARE, *block...  20.5 us
    all_to_all x1, starting transfers between devices, shards(): top = lax.all_to_all(top, everyone, 0, 0, tiled=True)  14.3 us
    ppermute x4, starting transfers between devices, neighbours(): return (lax.ppermute(last, axis, up), lax.ppermute(first, axis, down))  4.59 us
    pallas_call x1, Pallas kernels, call_prepare(): pl.pallas_call(prepare, out_shape=[layers, layers, turned, turned, jax.Sh...  3.31 us
  transfers between devices with their start and end apart: 5, of which 0 were waited for; matrix products, arithmetic and copies ran while one was open for 0% of the time, Pallas kernels for 26%

profile of v2, /device:TPU:131, one launch (start us, length us, event | category | flops | bytes accessed | tf_op | source)
XLA Modules:
  0.0 79.3 jit_solution(8797700453419123953)
XLA Ops:
  0.6 0.0 copy-start
  0.6 0.0 copy-start.1
  0.6 3.3 %prepare.1 = (f32[5,3,16,512]{3,2,1,0:T(8,128)}, f32[5,3,16,512]{3,2,1,0:T(8,128)}, f32[5,3,16,512]{3,2,1,0:T(8,128)}, f32[5,3,16,512]{3,2,1,0:T(8,128)}, f32[256,128]{1,0:T(8,128)}) custom-call(f32[5,16,16,512]{3,2,1,0:T(8,128)} %q_ref.3), custom_call_target="tpu_custom_call" | custom-call | flops 4000000 | bytes 5242880 | tf_op jit(solution)/shard_map/prepare/pallas_call | solution.py:493
  4.0 1.8 %collective-permute-start = (f32[5,3,16,512]{3,2,1,0:T(8,128)}, f32[5,3,16,512]{3,2,1,0:T(8,128)S(1)}, u32[]{:S(2)}, u32[]{:S(2)}) collective-permute-start(f32[5,3,16,512]{3,2,1,0:T(8,128)} %get-tuple-element.8), channel_id=1, source_target_pairs={{0,4},{4,8},{8,12},{12,16},{16,20},{20,24},{24,28},{28,32},{32,36}... | collective-permute-start | bytes 1474568 | tf_op jit(solution)/shard_map/ppermute | solution.py:563
  5.8 0.0 collective-permute-start.1
  5.8 1.3 %collective-permute-start.2 = (f32[5,3,16,512]{3,2,1,0:T(8,128)}, f32[5,3,16,512]{3,2,1,0:T(8,128)}, u32[]{:S(2)}, u32[]{:S(2)}) collective-permute-start(f32[5,3,16,512]{3,2,1,0:T(8,128)} %get-tuple-element.10), channel_id=1, source_target_pairs={{0,1},{1,2},{2,3},{3,0},{4,5},{5,6},{6,7},{7,4},{8,9},{9,10},{10,1... | collective-permute-start | bytes 1474568 | tf_op jit(solution)/shard_map/ppermute | solution.py:563
  7.1 1.4 %collective-permute-start.3 = (f32[5,3,16,512]{3,2,1,0:T(8,128)}, f32[5,3,16,512]{3,2,1,0:T(8,128)}, u32[]{:S(2)}, u32[]{:S(2)}) collective-permute-start(f32[5,3,16,512]{3,2,1,0:T(8,128)} %get-tuple-element.11), channel_id=1, source_target_pairs={{1,0},{2,1},{3,2},{0,3},{5,4},{6,5},{7,6},{4,7},{9,8},{10,9},{11,1... | collective-permute-start | bytes 1474568 | tf_op jit(solution)/shard_map/ppermute | solution.py:563
  8.6 14.3 %all-to-all-start = ((f32[256,1,128]{2,1,0:T(1,128)}), f32[256,1,128]{2,1,0:T(1,128)S(1)}, u32[]{:S(2)}, u32[]{:S(2)}) async-start(f32[256,1,128]{2,1,0:T(1,128)} %bitcast.5), calls=%async_computation | async-start | bytes 262144 | tf_op jit(solution)/shard_map/all_to_all | solution.py:571
  22.8 0.0 copy-done
  22.8 0.0 copy-done.1
  22.8 20.5 %along_lanes.1.za_ref.zb_ref = f32[14,8,5,8,16,128]{5,4,3,2,1,0:T(8,128)} custom-call(s32[1,1,32]{2,1,0:T(1,128)S(1)} %copy-done.1, f32[5,16,16,512]{3,2,1,0:T(8,128)S(1)} %copy-done), custom_call_target="tpu_custom_call" | custom-call | flops 120000000 | bytes 5242880 | tf_op jit(solution)/shard_map/along_lanes/pallas_call | solution.py:508
  43.3 0.0 all-to-all-done
  43.3 0.0 collective-permute-done.xl_ref
  43.3 0.0 collective-permute-done.1.xr_ref
  43.3 0.0 collective-permute-done.2.yl_ref
  43.4 0.0 collective-permute-done.3.yr_ref
  43.4 35.9 %along_others.1 = (f32[5,16,16,512]{3,2,1,0:T(8,128)}, f32[5,16,16,512]{3,2,1,0:T(8,128)}) custom-call(s32[1,1,32]{2,1,0:T(1,128)S(1)} %copy-done.1, f32[256,128]{1,0:T(8,128)S(1)} %bitcast.4, f32[5,16,16,512]{3,2,1,0:T(8,128)S(1)} %copy-done, f32[5,3,16,512]{3,2,1,0:T(8,128)S(1)} %collective-permute-done.xl_ref, ...), custom_call_target="tpu_custom_call" | custom-call | flops 240000000 | bytes 10485760 | tf_op jit(solution)/shard_map/along_others/pallas_call | solution.py:535
Async XLA Ops:
  0.6 22.2 %copy-start = (f32[5,16,16,512]{3,2,1,0:T(8,128)S(1)}, f32[5,16,16,512]{3,2,1,0:T(8,128)}, u32[]{:S(2)}) copy-start(f32[5,16,16,512]{3,2,1,0:T(8,128)} %q_ref.3) | copy-start | bytes 7864324
  0.6 22.2 %copy-start.1 = (s32[1,1,32]{2,1,0:T(1,128)S(1)}, s32[1,1,32]{2,1,0:T(1,128)}, u32[]{:S(2)}) copy-start(s32[1,1,32]{2,1,0:T(1,128)} %flag_ref.3) | copy-start | bytes 388
  4.0 39.4 %collective-permute-start = (f32[5,3,16,512]{3,2,1,0:T(8,128)}, f32[5,3,16,512]{3,2,1,0:T(8,128)S(1)}, u32[]{:S(2)}, u32[]{:S(2)}) collective-permute-start(f32[5,3,16,512]{3,2,1,0:T(8,128)} %get-tuple-element.8), channel_id=1, source_target_pairs={{0,4},{4,8},{8,12},{12,16},{16,20},{20,24},{24,28},{28,32},{32,36}... | collective-permute-start | bytes 1474568 | tf_op jit(solution)/shard_map/ppermute | solution.py:563
  5.8 37.5 %collective-permute-start.1 = (f32[5,3,16,512]{3,2,1,0:T(8,128)}, f32[5,3,16,512]{3,2,1,0:T(8,128)}, u32[]{:S(2)}, u32[]{:S(2)}) collective-permute-start(f32[5,3,16,512]{3,2,1,0:T(8,128)} %get-tuple-element.9), channel_id=1, source_target_pairs={{4,0},{8,4},{12,8},{16,12},{20,16},{24,20},{28,24},{32,28},{36,32}... | collective-permute-start | bytes 1474568 | tf_op jit(solution)/shard_map/ppermute | solution.py:563
  5.8 37.5 %collective-permute-start.2 = (f32[5,3,16,512]{3,2,1,0:T(8,128)}, f32[5,3,16,512]{3,2,1,0:T(8,128)}, u32[]{:S(2)}, u32[]{:S(2)}) collective-permute-start(f32[5,3,16,512]{3,2,1,0:T(8,128)} %get-tuple-element.10), channel_id=1, source_target_pairs={{0,1},{1,2},{2,3},{3,0},{4,5},{5,6},{6,7},{7,4},{8,9},{9,10},{10,1... | collective-permute-start | bytes 1474568 | tf_op jit(solution)/shard_map/ppermute | solution.py:563
  7.1 36.2 %collective-permute-start.3 = (f32[5,3,16,512]{3,2,1,0:T(8,128)}, f32[5,3,16,512]{3,2,1,0:T(8,128)}, u32[]{:S(2)}, u32[]{:S(2)}) collective-permute-start(f32[5,3,16,512]{3,2,1,0:T(8,128)} %get-tuple-element.11), channel_id=1, source_target_pairs={{1,0},{2,1},{3,2},{0,3},{5,4},{6,5},{7,6},{4,7},{9,8},{10,9},{11,1... | collective-permute-start | bytes 1474568 | tf_op jit(solution)/shard_map/ppermute | solution.py:563
  8.6 34.8 %all-to-all-start = ((f32[256,1,128]{2,1,0:T(1,128)}), f32[256,1,128]{2,1,0:T(1,128)S(1)}, u32[]{:S(2)}, u32[]{:S(2)}) async-start(f32[256,1,128]{2,1,0:T(1,128)} %bitcast.5), calls=%async_computation | async-start | bytes 262144 | tf_op jit(solution)/shard_map/all_to_all | solution.py:571
